TPU v7x, 512 devices: a whole 4x4x16 slice. The times are simulated.
512 devices in a mesh: sec: 16 (over z_lo, y), tile: 32 (over x, z_hi, core).
Axes of the slice: x: 4, y: 4, z: 16 (z_hi: 4, z_lo: 4; z = z_hi * 4 + z_lo), core: 2. Of those that a mesh axis runs over, the one named last changes fastest.
Arguments:
- snapshots: bfloat16 [5, 256, 3072, 256], P(None, 'sec', 'tile'), may hold values from -6 to 6
- eig_columns: bfloat16 [256, 256], P(None, 'tile'), may hold values from -0.375 to 0.375
- mean_u: float32 [256, 3072], P('sec', 'tile'), may hold values from 0.2 to 1
- mean_v: float32 [256, 3072], P('sec', 'tile'), may hold values from -0.5 to 0.5
- mean_rho: float32 [256, 3072], P('sec', 'tile'), may hold values from 0.5 to 2
- mean_shear: float32 [256, 3072], P('sec', 'tile'), may hold values from 0.2 to 2
- sound: float32 [256, 3072], P('sec', 'tile'), may hold values from 0.5 to 4
Outputs:
- rayleigh: float32 [16, 256, 256], P('sec', 'tile')
All inputs are finite; a program needn't handle non-finite values.
Results may differ from a plain program's by a relative error of at most 0.0044.
Values may be sent and summed in bfloat16 or wider, within the bound.
No kernel may reach another device: no remote copies, remote signals or barrier semaphores. Data moves between devices by JAX's collectives and lax.ppermute only.
A program may use at most 64 MiB of HBM per device.

v0:
```python
import jax
import jax.numpy as jnp
from jax import lax
from jax.sharding import PartitionSpec as P

viscosity = 0.002


def extended(cells, sides, width):
    for axis, dim in sides:
        count = lax.axis_size(axis)
        ends = count - 1
        head = lax.slice_in_dim(cells, 0, width, axis=dim)
        tail = lax.slice_in_dim(cells, cells.shape[dim] - width, cells.shape[dim], axis=dim)
        cells = jnp.concatenate(
            [
                lax.ppermute(tail, axis, [(i, (i + 1) % count) for i in range(ends)]),
                cells,
                lax.ppermute(head, axis, [((i + 1) % count, i) for i in range(ends)]),
            ],
            axis=dim,
        )
    return cells


def prefix(value, axis, join, neutral):
    count, mine = (lax.axis_size(axis), lax.axis_index(axis))
    pieces = lax.all_gather(value, axis)
    subtotal = jnp.full_like(value, 0) + jnp.asarray(neutral, value.dtype)

    def lap(position, subtotal):
        longer = join(subtotal, pieces[position])
        return jnp.where(position < mine, longer, subtotal)

    return lax.fori_loop(0, count - 1, lap, subtotal)


def field_at(padded, k, off_x, off_y):
    end_x = padded.shape[1] - 1 + off_x
    end_y = padded.shape[2] - 1 + off_y
    return padded[k, 1 + off_x : end_x, 1 + off_y : end_y, :].astype(jnp.float32)


def gradient(padded, k):
    along_x = (field_at(padded, k, 1, 0) - field_at(padded, k, -1, 0)) * 0.5
    along_y = (field_at(padded, k, 0, 1) - field_at(padded, k, 0, -1)) * 0.5
    return (along_x, along_y)


def laplace(padded, k):
    total = field_at(padded, k, 1, 0) + field_at(padded, k, -1, 0)
    total = total + field_at(padded, k, 0, 1) + field_at(padded, k, 0, -1)
    return total - 4.0 * field_at(padded, k, 0, 0)


def stencil(padded, mean_u, mean_v, mean_rho, mean_shear, sound):
    flow_x = mean_u[:, :, None]
    flow_y = mean_v[:, :, None]
    density = mean_rho[:, :, None]
    inverse = 1.0 / density
    shear = mean_shear[:, :, None]
    stiff = sound[:, :, None]
    rho_x, rho_y = gradient(padded, 0)
    u_x, u_y = gradient(padded, 1)
    v_x, v_y = gradient(padded, 2)
    w_x, w_y = gradient(padded, 3)
    p_x, p_y = gradient(padded, 4)
    diverge = u_x + v_y
    image_rho = -(flow_x * rho_x + flow_y * rho_y) - density * diverge
    image_u = (
        -(flow_x * u_x + flow_y * u_y)
        - shear * field_at(padded, 2, 0, 0)
        - inverse * p_x
        + viscosity * laplace(padded, 1)
    )
    image_v = -(flow_x * v_x + flow_y * v_y) - inverse * p_y + viscosity * laplace(padded, 2)
    image_w = -(flow_x * w_x + flow_y * w_y) + viscosity * laplace(padded, 3)
    image_p = -(flow_x * p_x + flow_y * p_y) - stiff * diverge
    return jnp.stack([image_rho, image_u, image_v, image_w, image_p]).astype(jnp.bfloat16)


def form_modes(block, piece):
    return jnp.einsum("fxys,sk->fxyk", block, piece, preferred_element_type=jnp.float32).astype(
        jnp.bfloat16
    )


def add_blocks(earlier, later):
    return earlier + later


def body(snapshots, eig_columns, mean_u, mean_v, mean_rho, mean_shear, sound):
    sections = lax.axis_size("sec")
    tiles_n = lax.axis_size("tile")
    cells_x = snapshots.shape[1]
    cells_y = snapshots.shape[2]
    scale = float(5 * cells_x * cells_y * sections * tiles_n) ** (-0.5)
    modes = form_modes(snapshots, lax.all_gather(eig_columns, "tile", axis=1, tiled=True))
    padded = extended(modes, (("sec", 1), ("tile", 2)), 1)
    image = stencil(padded, mean_u, mean_v, mean_rho, mean_shear, sound)
    own_rows = lax.psum_scatter(
        jnp.einsum("fxyk,fxyl->kl", modes, image, preferred_element_type=jnp.float32) * scale,
        "tile",
        scatter_dimension=0,
        tiled=True,
    )
    upstream = prefix(own_rows, "sec", add_blocks, jnp.zeros_like(own_rows))
    prefix_sum = upstream + own_rows
    return prefix_sum[None]


def solution(mesh):
    in_specs = (
        P(None, "sec", "tile", None),
        P(None, "tile"),
        P("sec", "tile"),
        P("sec", "tile"),
        P("sec", "tile"),
        P("sec", "tile"),
        P("sec", "tile"),
    )
    out_specs = P("sec", "tile", None)
    return jax.shard_map(body, mesh=mesh, in_specs=in_specs, out_specs=out_specs, check_vma=False)
```

profile of v0, /device:TPU:2, one launch (start us, length us, event | category | flops | bytes accessed | tf_op | source)
XLA Modules:
  0.0 275.3 jit_solution(12448692880432046577)
XLA Ops:
  6.5 0.0 reduce-scatter.2.cloned.1.call-start
  6.5 55.4 %all_gather.9 = bf16[256,256]{0,1:T(8,128)(2,1)S(1)} all-gather(bf16[256,8]{0,1:T(8,128)(2,1)} %param.10), channel_id=1, replica_groups=mesh['sec'=16,'tile'=32] {'tile'}, dimensions={1}, use_global_device_ids=true | all-gather | bytes 135168 | tf_op jit(solution)/shard_map/all_gather | solution.py:98
  61.9 0.0 copy-start.1
  61.9 0.0 copy-start.2
  61.9 3.4 %convolution_convert_fusion = bf16[5,16,96,256]{3,2,1,0:T(8,128)(2,1)S(1)} fusion(bf16[5,16,96,256]{3,2,1,0:T(8,128)(2,1)} %param.9, bf16[256,256]{0,1:T(8,128)(2,1)S(1)} %all_gather.9), kind=kOutput, calls=%fused_computation.1 | convolution fusion | flops 1008599040 | bytes 7995392 | tf_op jit(solution)/shard_map/fxys,sk->fxyk/dot_general | solution.py:83
  65.3 1.3 collective-permute-start
  66.6 4.6 %collective-permute-start.1 = (bf16[5,1,96,256]{3,2,1,0:T(8,128)(2,1)S(1)}, bf16[5,1,96,256]{3,2,1,0:T(8,128)(2,1)S(1)}, u32[]{:S(2)}, u32[]{:S(2)}) collective-permute-start(bf16[5,1,96,256]{3,2,1,0:T(8,128)(2,1)S(1)} %get-tuple-element.110), channel_id=1, source_target_pairs={{0,32},{32,64},{64,96},{96,128},{128,160},{160,192},{192,224},{224... | collective-permute-start | bytes 737288 | tf_op jit(solution)/shard_map/ppermute | solution.py:17
  71.2 0.0 copy-done.1
  71.2 0.0 copy-done.2
  71.2 0.0 copy-start.3
  71.2 0.0 copy-start.4
  71.2 4.2 %collective-permute-done = bf16[5,1,96,256]{3,2,1,0:T(8,128)(2,1)S(1)} collective-permute-done((bf16[5,1,96,256]{3,2,1,0:T(8,128)(2,1)S(1)}, bf16[5,1,96,256]{3,2,1,0:T(8,128)(2,1)S(1)}, u32[]{:S(2)}, u32[]{:S(2)}) %collective-permute-start) | collective-permute-done | bytes 245792 | tf_op jit(solution)/shard_map/ppermute | solution.py:19
  75.4 1.2 collective-permute-done.1
  76.6 0.1 pad_maximum_fusion.18
  76.7 4.2 %collective-permute-start.2 = (bf16[5,18,1,256]{3,2,1,0:T(2,128)(2,1)S(1)}, bf16[5,18,1,256]{3,2,1,0:T(2,128)(2,1)S(1)}, u32[]{:S(2)}, u32[]{:S(2)}) collective-permute-start(bf16[5,18,1,256]{3,2,1,0:T(2,128)(2,1)S(1)} %get-tuple-element.108), channel_id=1, source_target_pairs={{1,0},{2,1},{3,2},{4,3},{5,4},{6,5},{7,6},{8,7},{9,8},{10,9},{11,1... | collective-permute-start | bytes 138248 | tf_op jit(solution)/shard_map/ppermute | solution.py:19
  80.9 1.9 collective-permute-start.3
  82.9 0.0 copy-done.3
  82.9 0.0 copy-done.4
  82.9 0.2 collective-permute-done.2
  83.1 8.5 %collective-permute-done.3 = bf16[5,18,1,256]{3,2,1,0:T(2,128)(2,1)S(1)} collective-permute-done((bf16[5,18,1,256]{3,2,1,0:T(2,128)(2,1)S(1)}, bf16[5,18,1,256]{3,2,1,0:T(2,128)(2,1)S(1)}, u32[]{:S(2)}, u32[]{:S(2)}) %collective-permute-start.3) | collective-permute-done | bytes 46112 | tf_op jit(solution)/shard_map/ppermute | solution.py:17
  91.6 0.0 copy-start
  91.6 5.0 %fusion.27 = bf16[5,16,96,256]{3,2,1,0:T(8,128)(2,1)S(1)} fusion(bf16[5,18,1,256]{3,2,1,0:T(2,128)(2,1)S(1)} %collective-permute-done.3, bf16[5,1,96,256]{3,2,1,0:T(8,128)(2,1)S(1)} %collective-permute-done, bf16[5,16,96,256]{3,2,1,0:T(8,128)(2,1)S(1)} %convolution_convert_fusion, bf16[5,1,96,256]{3,2,1,0:T(8,128)(2,1)S(1)} %collective-permute-done.1, ...), kind=kLoop, calls=%fused_computation.51 | loop fusion | flops 23592960 | bytes 5320704
  96.6 0.0 copy-done
  96.6 2.6 fusion.30
  99.2 5.2 %fusion.31 = bf16[5,16,96,256]{3,2,1,0:T(8,128)(2,1)S(1)} fusion(bf16[5,16,96,256]{3,2,1,0:T(8,128)(2,1)S(1)} %fusion.30, bf16[5,16,96,256]{3,2,1,0:T(8,128)(2,1)S(1)} %convolution_convert_fusion, bf16[5,1,96,256]{3,2,1,0:T(8,128)(2,1)S(1)} %collective-permute-done.1, bf16[5,1,96,256]{3,2,1,0:T(8,128)(2,1)S(1)} %collective-permute-done, ...), kind=kLoop, calls=%fused_computation.55 | loop fusion | flops 22806528 | bytes 6205440
  104.5 2.1 fusion.29
  106.6 5.7 %fusion.28 = bf16[5,16,96,256]{3,2,1,0:T(8,128)(2,1)S(1)} fusion(bf16[5,16,96,256]{3,2,1,0:T(8,128)(2,1)S(1)} %fusion.29, f32[16,96]{1,0:T(8,128)S(1)} %get-tuple-element.115, f32[16,96]{1,0:T(8,128)S(1)} %get-tuple-element.114, f32[16,96]{1,0:T(8,128)S(1)} %get-tuple-element.116, bf16[5,1,96,256]{3,2,1,0:T(8,128)(2,1)S(1)} %collective-permute-done, ...), kind=kLoop, calls=%fused_computation.52 | loop fusion | flops 23592960 | bytes 5419008 | tf_op jit(solution)/shard_map/stack | solution.py:79
  112.3 1.9 fusion.26
  114.2 0.0 reduce-scatter.2.cloned.1.call-update
  114.3 110.3 %reduce-scatter.2.cloned.1.call-done = f32[8,256]{1,0:T(8,128)} async-done(((f32[256,256]{1,0:T(8,128)}), f32[8,256]{1,0:T(8,128)}) %reduce-scatter.2.cloned.1.call-update) | async-done | bytes 8208 | tf_op jit(solution)/shard_map/reduce_scatter | solution.py:101
  224.6 42.1 %all-gather = f32[128,256]{1,0:T(8,128)S(1)} all-gather(f32[8,256]{1,0:T(8,128)} %reduce-scatter.2.cloned.1.call-done), channel_id=2, replica_groups=mesh['sec'=16,'tile'=32] {'sec'}, dimensions={0}, use_global_device_ids=true | all-gather | bytes 139264 | tf_op jit(solution)/shard_map/all_gather | solution.py:28
  266.7 0.5 while.14
  267.2 1.3 add_bitcast_fusion
  (19 shorter events, 0.2 us)
Async XLA Ops:
  6.5 218.1 %reduce-scatter.2.cloned.1.call-start = ((), (), s32[]{:S(2)}) async-start(), calls=%async_computation.1 | async-start | bytes 270336 | tf_op jit(solution)/shard_map/reduce_scatter | solution.py:101
  61.9 9.3 %copy-start.1 = (f32[16,96]{1,0:T(8,128)S(1)}, f32[16,96]{1,0:T(8,128)}, u32[]{:S(2)}) copy-start(f32[16,96]{1,0:T(8,128)} %param.13) | copy-start | bytes 18436
  61.9 9.3 %copy-start.2 = (f32[16,96]{1,0:T(8,128)S(1)}, f32[16,96]{1,0:T(8,128)}, u32[]{:S(2)}) copy-start(f32[16,96]{1,0:T(8,128)} %param.12) | copy-start | bytes 18436
  65.3 10.1 %collective-permute-start = (bf16[5,1,96,256]{3,2,1,0:T(8,128)(2,1)S(1)}, bf16[5,1,96,256]{3,2,1,0:T(8,128)(2,1)S(1)}, u32[]{:S(2)}, u32[]{:S(2)}) collective-permute-start(bf16[5,1,96,256]{3,2,1,0:T(8,128)(2,1)S(1)} %get-tuple-element.111), channel_id=1, source_target_pairs={{32,0},{64,32},{96,64},{128,96},{160,128},{192,160},{224,192},{256... | collective-permute-start | bytes 737288 | tf_op jit(solution)/shard_map/ppermute | solution.py:19
  66.6 10.0 %collective-permute-start.1 = (bf16[5,1,96,256]{3,2,1,0:T(8,128)(2,1)S(1)}, bf16[5,1,96,256]{3,2,1,0:T(8,128)(2,1)S(1)}, u32[]{:S(2)}, u32[]{:S(2)}) collective-permute-start(bf16[5,1,96,256]{3,2,1,0:T(8,128)(2,1)S(1)} %get-tuple-element.110), channel_id=1, source_target_pairs={{0,32},{32,64},{64,96},{96,128},{128,160},{160,192},{192,224},{224... | collective-permute-start | bytes 737288 | tf_op jit(solution)/shard_map/ppermute | solution.py:17
  71.2 11.7 %copy-start.3 = (f32[16,96]{1,0:T(8,128)S(1)}, f32[16,96]{1,0:T(8,128)}, u32[]{:S(2)}) copy-start(f32[16,96]{1,0:T(8,128)} %param.15) | copy-start | bytes 18436
  71.2 11.7 %copy-start.4 = (f32[16,96]{1,0:T(8,128)S(1)}, f32[16,96]{1,0:T(8,128)}, u32[]{:S(2)}) copy-start(f32[16,96]{1,0:T(8,128)} %param.11) | copy-start | bytes 18436
  76.7 6.3 %collective-permute-start.2 = (bf16[5,18,1,256]{3,2,1,0:T(2,128)(2,1)S(1)}, bf16[5,18,1,256]{3,2,1,0:T(2,128)(2,1)S(1)}, u32[]{:S(2)}, u32[]{:S(2)}) collective-permute-start(bf16[5,18,1,256]{3,2,1,0:T(2,128)(2,1)S(1)} %get-tuple-element.108), channel_id=1, source_target_pairs={{1,0},{2,1},{3,2},{4,3},{5,4},{6,5},{7,6},{8,7},{9,8},{10,9},{11,1... | collective-permute-start | bytes 138248 | tf_op jit(solution)/shard_map/ppermute | solution.py:19
  80.9 10.7 %collective-permute-start.3 = (bf16[5,18,1,256]{3,2,1,0:T(2,128)(2,1)S(1)}, bf16[5,18,1,256]{3,2,1,0:T(2,128)(2,1)S(1)}, u32[]{:S(2)}, u32[]{:S(2)}) collective-permute-start(bf16[5,18,1,256]{3,2,1,0:T(2,128)(2,1)S(1)} %get-tuple-element.109), channel_id=1, source_target_pairs={{0,1},{1,2},{2,3},{3,4},{4,5},{5,6},{6,7},{7,8},{8,9},{9,10},{10,1... | collective-permute-start | bytes 138248 | tf_op jit(solution)/shard_map/ppermute | solution.py:17
  91.6 5.0 %copy-start = (f32[16,96]{1,0:T(8,128)S(1)}, f32[16,96]{1,0:T(8,128)}, u32[]{:S(2)}) copy-start(f32[16,96]{1,0:T(8,128)} %param.14) | copy-start | bytes 18436
Sparse Core Ops, SparseCore 0:
  114.4 110.1 reduce-scatter.1
where the time goes:
time: 276 us; the launch traced here: 275 us
  waiting for transfers between devices  124 us (45%)
  blocking collectives  97.4 us (35%)
  other arithmetic  22.2 us (8%)
  between operations  13.6 us (5%)
  starting transfers between devices  12 us (4%)
  matrix products  5.3 us (2%)
    reduce_scatter x1, waiting for transfers between devices, body(): lax.psum_scatter(jnp.einsum('fxyk,fxyl->kl', modes, image, preferred_elem...  110 us
    all_gather x1, blocking collectives, body(): lax.all_gather(eig_columns, 'tile', axis=1, tiled=True)  55.4 us
    all_gather x1, blocking collectives, prefix(): pieces = lax.all_gather(value, axis)  42.1 us
    unnamed x5, other arithmetic  14.9 us
    ppermute x2, waiting for transfers between devices, extended(): lax.ppermute(tail, axis, [(i, (i + 1) % count) for i in range(ends)])  9.72 us
    ppermute x2, starting transfers between devices, extended(): lax.ppermute(tail, axis, [(i, (i + 1) % count) for i in range(ends)])  6.48 us
    another operation x1, other arithmetic, stencil(): jnp.stack([image_rho, image_u, image_v, image_w, image_p])  5.68 us
  transfers between devices with their start and end apart: 5, of which 5 were waited for; matrix products, arithmetic and copies ran while one was open for 0% of the time, Pallas kernels for 0%

commit v1 on v0

--- a/solution.py
+++ b/solution.py
@@ -95,7 +95,12 @@
     cells_x = snapshots.shape[1]
     cells_y = snapshots.shape[2]
     scale = float(5 * cells_x * cells_y * sections * tiles_n) ** (-0.5)
-    modes = form_modes(snapshots, lax.all_gather(eig_columns, "tile", axis=1, tiled=True))
+    modes = form_modes(
+        snapshots,
+        jnp.concatenate(
+            lax.all_to_all(jnp.stack([eig_columns] * lax.axis_size("tile")), "tile", 0, 0), axis=1
+        ),
+    )
     padded = extended(modes, (("sec", 1), ("tile", 2)), 1)
     image = stencil(padded, mean_u, mean_v, mean_rho, mean_shear, sound)
     own_rows = lax.psum_scatter(

time: 276 us -> 254 us (0.920)
  blocking collectives: 97.4 us -> 74.5 us
    all_gather x1 -> x0, blocking collectives: 55.4 us -> none  [body(): lax.all_gather(eig_columns, 'tile', axis=1, tiled=True)]
    all_to_all x0 -> x1, blocking collectives: none -> 32.4 us  [body(): lax.all_to_all(jnp.stack([eig_columns] * lax.axis_size('tile')), 'tile',...]
where the time goes in v1:
time: 254 us
  waiting for transfers between devices  126 us (50%)
  blocking collectives  74.5 us (29%)
  other arithmetic  22.2 us (9%)
  between operations  13.6 us (5%)
  starting transfers between devices  10.7 us (4%)
  matrix products  5.3 us (2%)
    reduce_scatter x1, waiting for transfers between devices, body(): lax.psum_scatter(jnp.einsum('fxyk,fxyl->kl', modes, image, preferred_elem...  112 us
    all_gather x1, blocking collectives, prefix(): pieces = lax.all_gather(value, axis)  42.1 us
    all_to_all x1, blocking collectives, body(): lax.all_to_all(jnp.stack([eig_columns] * lax.axis_size('tile')), 'tile',...  32.4 us
    unnamed x5, other arithmetic  14.9 us
    ppermute x2, waiting for transfers between devices, extended(): lax.ppermute(tail, axis, [(i, (i + 1) % count) for i in range(ends)])  10.3 us
    ppermute x2, starting transfers between devices, extended(): lax.ppermute(tail, axis, [(i, (i + 1) % count) for i in range(ends)])  6.48 us
    another operation x1, other arithmetic, stencil(): jnp.stack([image_rho, image_u, image_v, image_w, image_p])  5.68 us
  transfers between devices with their start and end apart: 5, of which 5 were waited for; matrix products, arithmetic and copies ran while one was open for 0% of the time, Pallas kernels for 0%

profile of v1, /device:TPU:2, one launch (start us, length us, event | category | flops | bytes accessed | tf_op | source)
XLA Modules:
  0.0 253.7 jit_solution(12426162331017223167)
XLA Ops:
  6.5 0.0 reduce-scatter.2.cloned.1.call-start
  6.5 0.7 stack.5
  7.2 32.4 %all_to_all.5 = bf16[32,256,8]{1,2,0:T(8,128)(2,1)S(1)} all-to-all(bf16[32,256,8]{1,2,0:T(8,128)(2,1)S(1)} %stack.5), channel_id=1, replica_groups=mesh['sec'=16,'tile'=32] {'tile'}, dimensions={0} | all-to-all | bytes 262144 | tf_op jit(solution)/shard_map/all_to_all | solution.py:101
  39.6 0.0 copy-start.1
  39.6 0.0 copy-start.2
  39.6 3.4 %convolution_convert_fusion = bf16[5,16,96,256]{3,2,1,0:T(8,128)(2,1)S(1)} fusion(bf16[5,16,96,256]{3,2,1,0:T(8,128)(2,1)} %param.9, bf16[32,256,8]{1,2,0:T(8,128)(2,1)S(1)} %all_to_all.5), kind=kOutput, calls=%fused_computation.1 | convolution fusion | flops 1008599040 | bytes 7995392 | tf_op jit(solution)/shard_map/fxys,sk->fxyk/dot_general | solution.py:83
  43.0 1.3 collective-permute-start
  44.3 4.6 %collective-permute-start.1 = (bf16[5,1,96,256]{3,2,1,0:T(8,128)(2,1)S(1)}, bf16[5,1,96,256]{3,2,1,0:T(8,128)(2,1)S(1)}, u32[]{:S(2)}, u32[]{:S(2)}) collective-permute-start(bf16[5,1,96,256]{3,2,1,0:T(8,128)(2,1)S(1)} %get-tuple-element.110), channel_id=1, source_target_pairs={{0,32},{32,64},{64,96},{96,128},{128,160},{160,192},{192,224},{224... | collective-permute-start | bytes 737288 | tf_op jit(solution)/shard_map/ppermute | solution.py:17
  48.9 0.0 copy-done.1
  48.9 0.0 copy-done.2
  49.0 0.0 copy-start.3
  49.0 0.0 copy-start.4
  49.0 4.1 %collective-permute-done = bf16[5,1,96,256]{3,2,1,0:T(8,128)(2,1)S(1)} collective-permute-done((bf16[5,1,96,256]{3,2,1,0:T(8,128)(2,1)S(1)}, bf16[5,1,96,256]{3,2,1,0:T(8,128)(2,1)S(1)}, u32[]{:S(2)}, u32[]{:S(2)}) %collective-permute-start) | collective-permute-done | bytes 245792 | tf_op jit(solution)/shard_map/ppermute | solution.py:19
  53.1 1.7 collective-permute-done.1
  54.8 0.1 pad_maximum_fusion.18
  55.0 3.0 %collective-permute-start.2 = (bf16[5,18,1,256]{3,2,1,0:T(2,128)(2,1)S(1)}, bf16[5,18,1,256]{3,2,1,0:T(2,128)(2,1)S(1)}, u32[]{:S(2)}, u32[]{:S(2)}) collective-permute-start(bf16[5,18,1,256]{3,2,1,0:T(2,128)(2,1)S(1)} %get-tuple-element.108), channel_id=1, source_target_pairs={{1,0},{2,1},{3,2},{4,3},{5,4},{6,5},{7,6},{8,7},{9,8},{10,9},{11,1... | collective-permute-start | bytes 138248 | tf_op jit(solution)/shard_map/ppermute | solution.py:19
  57.9 1.9 collective-permute-start.3
  59.9 0.0 copy-done.3
  59.9 0.0 copy-done.4
  59.9 0.2 collective-permute-done.2
  60.1 8.5 %collective-permute-done.3 = bf16[5,18,1,256]{3,2,1,0:T(2,128)(2,1)S(1)} collective-permute-done((bf16[5,18,1,256]{3,2,1,0:T(2,128)(2,1)S(1)}, bf16[5,18,1,256]{3,2,1,0:T(2,128)(2,1)S(1)}, u32[]{:S(2)}, u32[]{:S(2)}) %collective-permute-start.3) | collective-permute-done | bytes 46112 | tf_op jit(solution)/shard_map/ppermute | solution.py:17
  68.6 0.0 copy-start
  68.6 5.0 %fusion.27 = bf16[5,16,96,256]{3,2,1,0:T(8,128)(2,1)S(1)} fusion(bf16[5,18,1,256]{3,2,1,0:T(2,128)(2,1)S(1)} %collective-permute-done.3, bf16[5,1,96,256]{3,2,1,0:T(8,128)(2,1)S(1)} %collective-permute-done, bf16[5,16,96,256]{3,2,1,0:T(8,128)(2,1)S(1)} %convolution_convert_fusion, bf16[5,1,96,256]{3,2,1,0:T(8,128)(2,1)S(1)} %collective-permute-done.1, ...), kind=kLoop, calls=%fused_computation.51 | loop fusion | flops 23592960 | bytes 5320704
  73.6 0.0 copy-done
  73.6 2.6 %fusion.30 = bf16[5,16,96,256]{3,2,1,0:T(8,128)(2,1)S(1)} fusion(bf16[5,16,96,256]{3,2,1,0:T(8,128)(2,1)S(1)} %fusion.27, bf16[5,16,96,256]{3,2,1,0:T(8,128)(2,1)S(1)} %convolution_convert_fusion, bf16[5,18,1,256]{3,2,1,0:T(2,128)(2,1)S(1)} %collective-permute-done.3, bf16[5,1,96,256]{3,2,1,0:T(8,128)(2,1)S(1)} %collective-permute-done, ...), kind=kLoop, calls=%fused_computation.54 | loop fusion | flops 20840448 | bytes 7000064
  76.2 5.2 %fusion.31 = bf16[5,16,96,256]{3,2,1,0:T(8,128)(2,1)S(1)} fusion(bf16[5,16,96,256]{3,2,1,0:T(8,128)(2,1)S(1)} %fusion.30, bf16[5,16,96,256]{3,2,1,0:T(8,128)(2,1)S(1)} %convolution_convert_fusion, bf16[5,1,96,256]{3,2,1,0:T(8,128)(2,1)S(1)} %collective-permute-done.1, bf16[5,1,96,256]{3,2,1,0:T(8,128)(2,1)S(1)} %collective-permute-done, ...), kind=kLoop, calls=%fused_computation.55 | loop fusion | flops 22806528 | bytes 6205440
  81.5 2.1 fusion.29
  83.6 5.7 %fusion.28 = bf16[5,16,96,256]{3,2,1,0:T(8,128)(2,1)S(1)} fusion(bf16[5,16,96,256]{3,2,1,0:T(8,128)(2,1)S(1)} %fusion.29, f32[16,96]{1,0:T(8,128)S(1)} %get-tuple-element.115, f32[16,96]{1,0:T(8,128)S(1)} %get-tuple-element.114, f32[16,96]{1,0:T(8,128)S(1)} %get-tuple-element.116, bf16[5,1,96,256]{3,2,1,0:T(8,128)(2,1)S(1)} %collective-permute-done, ...), kind=kLoop, calls=%fused_computation.52 | loop fusion | flops 23592960 | bytes 5419008 | tf_op jit(solution)/shard_map/stack | solution.py:79
  89.3 1.9 fusion.26
  91.2 0.0 reduce-scatter.2.cloned.1.call-update
  91.3 111.7 %reduce-scatter.2.cloned.1.call-done = f32[8,256]{1,0:T(8,128)} async-done(((f32[256,256]{1,0:T(8,128)}), f32[8,256]{1,0:T(8,128)}) %reduce-scatter.2.cloned.1.call-update) | async-done | bytes 8208 | tf_op jit(solution)/shard_map/reduce_scatter | solution.py:106
  202.9 42.1 %all-gather = f32[128,256]{1,0:T(8,128)S(1)} all-gather(f32[8,256]{1,0:T(8,128)} %reduce-scatter.2.cloned.1.call-done), channel_id=2, replica_groups=mesh['sec'=16,'tile'=32] {'sec'}, dimensions={0}, use_global_device_ids=true | all-gather | bytes 139264 | tf_op jit(solution)/shard_map/all_gather | solution.py:28
  245.0 0.5 while.14
  245.5 1.3 add_bitcast_fusion
  (19 shorter events, 0.2 us)
Async XLA Ops:
  6.5 196.4 %reduce-scatter.2.cloned.1.call-start = ((), (), s32[]{:S(2)}) async-start(), calls=%async_computation.2 | async-start | bytes 270336 | tf_op jit(solution)/shard_map/reduce_scatter | solution.py:106
  39.6 9.3 %copy-start.1 = (f32[16,96]{1,0:T(8,128)S(1)}, f32[16,96]{1,0:T(8,128)}, u32[]{:S(2)}) copy-start(f32[16,96]{1,0:T(8,128)} %param.13) | copy-start | bytes 18436
  39.6 9.3 %copy-start.2 = (f32[16,96]{1,0:T(8,128)S(1)}, f32[16,96]{1,0:T(8,128)}, u32[]{:S(2)}) copy-start(f32[16,96]{1,0:T(8,128)} %param.12) | copy-start | bytes 18436
  43.0 10.0 %collective-permute-start = (bf16[5,1,96,256]{3,2,1,0:T(8,128)(2,1)S(1)}, bf16[5,1,96,256]{3,2,1,0:T(8,128)(2,1)S(1)}, u32[]{:S(2)}, u32[]{:S(2)}) collective-permute-start(bf16[5,1,96,256]{3,2,1,0:T(8,128)(2,1)S(1)} %get-tuple-element.111), channel_id=1, source_target_pairs={{32,0},{64,32},{96,64},{128,96},{160,128},{192,160},{224,192},{256... | collective-permute-start | bytes 737288 | tf_op jit(solution)/shard_map/ppermute | solution.py:19
  44.3 10.5 %collective-permute-start.1 = (bf16[5,1,96,256]{3,2,1,0:T(8,128)(2,1)S(1)}, bf16[5,1,96,256]{3,2,1,0:T(8,128)(2,1)S(1)}, u32[]{:S(2)}, u32[]{:S(2)}) collective-permute-start(bf16[5,1,96,256]{3,2,1,0:T(8,128)(2,1)S(1)} %get-tuple-element.110), channel_id=1, source_target_pairs={{0,32},{32,64},{64,96},{96,128},{128,160},{160,192},{192,224},{224... | collective-permute-start | bytes 737288 | tf_op jit(solution)/shard_map/ppermute | solution.py:17
  49.0 10.9 %copy-start.3 = (f32[16,96]{1,0:T(8,128)S(1)}, f32[16,96]{1,0:T(8,128)}, u32[]{:S(2)}) copy-start(f32[16,96]{1,0:T(8,128)} %param.15) | copy-start | bytes 18436
  49.0 10.9 %copy-start.4 = (f32[16,96]{1,0:T(8,128)S(1)}, f32[16,96]{1,0:T(8,128)}, u32[]{:S(2)}) copy-start(f32[16,96]{1,0:T(8,128)} %param.11) | copy-start | bytes 18436
  55.0 5.1 %collective-permute-start.2 = (bf16[5,18,1,256]{3,2,1,0:T(2,128)(2,1)S(1)}, bf16[5,18,1,256]{3,2,1,0:T(2,128)(2,1)S(1)}, u32[]{:S(2)}, u32[]{:S(2)}) collective-permute-start(bf16[5,18,1,256]{3,2,1,0:T(2,128)(2,1)S(1)} %get-tuple-element.108), channel_id=1, source_target_pairs={{1,0},{2,1},{3,2},{4,3},{5,4},{6,5},{7,6},{8,7},{9,8},{10,9},{11,1... | collective-permute-start | bytes 138248 | tf_op jit(solution)/shard_map/ppermute | solution.py:19
  57.9 10.7 %collective-permute-start.3 = (bf16[5,18,1,256]{3,2,1,0:T(2,128)(2,1)S(1)}, bf16[5,18,1,256]{3,2,1,0:T(2,128)(2,1)S(1)}, u32[]{:S(2)}, u32[]{:S(2)}) collective-permute-start(bf16[5,18,1,256]{3,2,1,0:T(2,128)(2,1)S(1)} %get-tuple-element.109), channel_id=1, source_target_pairs={{0,1},{1,2},{2,3},{3,4},{4,5},{5,6},{6,7},{7,8},{8,9},{9,10},{10,1... | collective-permute-start | bytes 138248 | tf_op jit(solution)/shard_map/ppermute | solution.py:17
  68.6 5.0 %copy-start = (f32[16,96]{1,0:T(8,128)S(1)}, f32[16,96]{1,0:T(8,128)}, u32[]{:S(2)}) copy-start(f32[16,96]{1,0:T(8,128)} %param.14) | copy-start | bytes 18436
Sparse Core Ops, SparseCore 0:
  91.4 111.5 reduce-scatter.1
